TPU v7x, 256 devices: a whole 4x4x8 slice. The times are simulated.
256 devices in a mesh: ctx: 32 (over z, y), tp: 8 (over x, core).
Axes of the slice: x: 4, y: 4, z: 8, core: 2. Of those that a mesh axis runs over, the one named last changes fastest.
Arguments:
- tokens: bfloat16 [24576, 4096], P(('ctx', 'tp')), may hold values from -6 to 6
- norm_gain: float32 [4096], replicated, may hold values from 0.1 to 1.9
- w_qkv: bfloat16 [4096, 8192], P('ctx', 'tp'), may hold values from -0.09375 to 0.09375
- w_out: bfloat16 [4096, 4096], P('tp', 'ctx'), may hold values from -0.09375 to 0.09375
- head_gain: float32 [4096], P('tp'), may hold values from 0.1 to 1.9
- input_codes: int32 [8, 24576], P('tp', 'ctx'), may hold values from -4 to 4
- forget_codes: int32 [8, 24576], P('tp', 'ctx'), may hold values from -24 to 4
- forget_bias: float32 [8], P('tp'), may hold values from 3 to 13.5, as said below
- document_begin_flags: int32 [24576], P('ctx'), may hold values 0 or 1
Outputs:
- mixed: bfloat16 [24576, 4096], P(('ctx', 'tp'))
Inputs may be any that keep to these rules, and one draw needn't show every extreme that they name: `forget_bias`: a bias for each head.
All inputs are finite; a program needn't handle non-finite values. No bound on the sum of `document_begin_flags` on one device may be relied on, other than what follows from the above.
Results may differ from a plain program's by a relative error of at most 0.017.
Values may be sent and summed in bfloat16 or wider, within the bound.
A program may use at most 64 MiB of HBM per device.

v0:
```python
import jax
import jax.numpy as jnp
from jax import lax
from jax.sharding import PartitionSpec as P

DK = 256
DV = 512
EPSILON = 1e-06
FORGET_STEP = 0.5
INPUT_STEP = 0.5


def carried_in(passing, state, axis):
    count = lax.axis_size(axis)
    if count == 1:
        return jnp.zeros_like(state)
    heads, rows, width = state.shape
    pad = 16

    def shifted(decay, total, k):
        high = decay.astype(jnp.bfloat16)
        low = (decay - high.astype(jnp.float32)).astype(jnp.bfloat16)
        extra = jnp.zeros((heads, pad, width), jnp.bfloat16)
        extra = extra.at[:, 0, 0].set(high).at[:, 0, 1].set(low)
        message = jnp.concatenate([total.astype(jnp.bfloat16), extra], axis=1)
        pairs = [(i, i + k) for i in range(count - k)]
        got = lax.ppermute(message, axis, pairs)
        got_decay = got[:, rows, 0].astype(jnp.float32) + got[:, rows, 1].astype(jnp.float32)
        return (got_decay, got[:, :rows].astype(jnp.float32))

    decay, total = shifted(passing, state, 1)
    if count > 2:
        decay_far, total_far = shifted(passing, state, 2)
        total = decay[:, None, None] * total_far + total
        decay = decay * decay_far
    k = 2
    while k < count:
        decay_far, total_far = shifted(decay, total, k)
        total = decay[:, None, None] * total_far + total
        decay = decay * decay_far
        k *= 2
    return total


def rms_rows(embedded_entries, norm_gain):
    token_float = embedded_entries.astype(jnp.float32)
    moment = jnp.mean(token_float * token_float, axis=1, keepdims=True)
    return (token_float * lax.rsqrt(moment + EPSILON) * norm_gain).astype(jnp.bfloat16)


def local_terms(queries, key_rows, values, log_forget, input_gate, starts):
    length = queries.shape[0]
    scaling = queries.shape[1] ** (-0.5)
    segment = jnp.cumsum(starts)
    levels = jnp.cumsum(log_forget)
    position = jnp.arange(length)
    allowed = (position[:, None] >= position[None, :]) & (segment[:, None] == segment[None, :])
    decays = jnp.where(
        allowed,
        jnp.exp(jnp.minimum(levels[:, None] - levels[None, :], 0.0) + input_gate[None, :]),
        0.0,
    )
    scores = jnp.dot(queries, key_rows.T, preferred_element_type=jnp.float32) * scaling
    weights = (scores * decays).astype(jnp.bfloat16)
    inner_part = jnp.dot(weights, values, preferred_element_type=jnp.float32)
    last_level = levels[-1]
    last_seg = segment[-1]
    keeping = jnp.where(segment == last_seg, jnp.exp(last_level - levels + input_gate), 0.0)
    weighted = (key_rows.astype(jnp.float32) * keeping[:, None]).astype(jnp.bfloat16)
    local_state = lax.dot_general(
        weighted, values, (((0,), (0,)), ((), ())), preferred_element_type=jnp.float32
    )
    passing = jnp.where(last_seg == 0, jnp.exp(last_level), 0.0)
    carried = jnp.where(segment == 0, jnp.exp(levels), 0.0) * scaling
    return (inner_part, local_state, passing, carried)


def apply_state(queries, carried, incoming):
    lifted = queries.astype(jnp.float32) * carried[:, None]
    return jnp.dot(
        lifted, incoming, precision=lax.Precision.HIGHEST, preferred_element_type=jnp.float32
    )


def head_norm(head_out, gain):
    centre = jnp.mean(head_out, axis=1, keepdims=True)
    shifted = head_out - centre
    spread = jnp.mean(shifted * shifted, axis=1, keepdims=True)
    return (shifted * lax.rsqrt(spread + EPSILON) * gain).astype(jnp.bfloat16)


def local(
    tokens,
    norm_gain,
    w_qkv,
    w_out,
    head_gain,
    input_codes,
    forget_codes,
    forget_bias,
    document_begin_flags,
):
    normed = rms_rows(tokens, norm_gain)
    group = lax.axis_size("tp")
    copies = jnp.broadcast_to(normed[None], (group,) + normed.shape)
    every_row_list = lax.all_to_all(copies, "tp", 0, 0, tiled=True).reshape(-1, normed.shape[1])
    parameter_collection = lax.all_gather(w_qkv, "ctx", axis=0, tiled=True)
    rows_combined = jnp.dot(
        every_row_list, parameter_collection, preferred_element_type=jnp.float32
    )
    rows_combined = rows_combined.astype(jnp.bfloat16)
    heads_here = forget_bias.shape[0]
    stride = 2 * DK + DV
    query_list, inner_list, state_list, passing_list, carried_list = ([], [], [], [], [])
    attention_slot_number = 0
    offset = attention_slot_number * stride
    queries = rows_combined[:, offset : offset + DK]
    key_rows = rows_combined[:, offset + DK : offset + 2 * DK]
    values = rows_combined[:, offset + 2 * DK : offset + stride]
    log_forget = jax.nn.log_sigmoid(
        FORGET_STEP * forget_codes[attention_slot_number].astype(jnp.float32)
        + forget_bias[attention_slot_number]
    )
    input_gate = INPUT_STEP * input_codes[attention_slot_number].astype(jnp.float32)
    inner_part, local_state, passing, carried = local_terms(
        queries, key_rows, values, log_forget, input_gate, document_begin_flags
    )
    query_list.append(queries)
    inner_list.append(inner_part)
    state_list.append(local_state)
    passing_list.append(passing)
    carried_list.append(carried)
    incoming = carried_in(jnp.stack(passing_list), jnp.stack(state_list), "ctx")
    attention_slot_number = 0
    head_out = inner_list[attention_slot_number] + apply_state(
        query_list[attention_slot_number],
        carried_list[attention_slot_number],
        incoming[attention_slot_number],
    )
    normed_heads = head_norm(head_out, head_gain)
    out_columns = lax.all_gather(w_out, "ctx", axis=1, tiled=True)
    summed = lax.psum_scatter(
        jnp.dot(normed_heads, out_columns, preferred_element_type=jnp.float32).astype(jnp.bfloat16),
        "tp",
        scatter_dimension=0,
        tiled=True,
    ).astype(jnp.float32)
    return (tokens.astype(jnp.float32) + summed).astype(jnp.bfloat16)


def solution(mesh):
    placed = (
        P(("ctx", "tp"), None),
        P(),
        P("ctx", "tp"),
        P("tp", "ctx"),
        P("tp"),
        P("tp", "ctx"),
        P("tp", "ctx"),
        P("tp"),
        P("ctx"),
    )
    return jax.shard_map(
        local, mesh=mesh, in_specs=placed, out_specs=P(("ctx", "tp"), None), check_vma=False
    )
```

profile of v0, /device:TPU:1, one launch (start us, length us, event | category | flops | bytes accessed | tf_op | source)
XLA Modules:
  0.0 284.2 jit_solution(16675667116050032039)
XLA Ops:
  7.3 1.4 fusion.1
  9.7 3.3 %broadcast_in_dim.5 = bf16[8,96,4096]{2,1,0:T(8,128)(2,1)} broadcast(bf16[96,4096]{1,0:T(8,128)(2,1)S(1)} %fusion.3), dimensions={1,2} | broadcast | bytes 7077888 | tf_op jit(solution)/shard_map/broadcast_in_dim | solution.py:105
  13.0 8.0 %all-to-all-start = ((bf16[8,96,4096]{2,1,0:T(8,128)(2,1)}), bf16[8,96,4096]{2,1,0:T(8,128)(2,1)}, u32[]{:S(2)}, u32[]{:S(2)}) async-start(bf16[8,96,4096]{2,1,0:T(8,128)(2,1)} %broadcast_in_dim.5), calls=%async_computation | async-start | bytes 12582912 | tf_op jit(solution)/shard_map/all_to_all | solution.py:106
  29.4 63.0 %all-to-all-done = bf16[8,96,4096]{2,1,0:T(8,128)(2,1)} async-done(((bf16[8,96,4096]{2,1,0:T(8,128)(2,1)}), bf16[8,96,4096]{2,1,0:T(8,128)(2,1)}, u32[]{:S(2)}, u32[]{:S(2)}) %all-to-all-start) | async-done | bytes 6291488 | tf_op jit(solution)/shard_map/all_to_all | solution.py:106
  92.5 19.3 %all-gather.3.cloned.1.call-done = bf16[4096,1024]{1,0:T(8,128)(2,1)} async-done(((bf16[128,1024]{1,0:T(8,128)(2,1)}), bf16[4096,1024]{1,0:T(8,128)(2,1)}) %all-gather.3.cloned.1.call-update) | async-done | bytes 8388624 | tf_op jit(solution)/shard_map/all_gather | solution.py:107
  111.7 10.9 %convolution_convert_fusion.1 = bf16[768,1024]{1,0:T(8,128)(2,1)S(1)} fusion(bf16[768,4096]{1,0:T(8,128)(2,1)} %bitcast, bf16[4096,1024]{1,0:T(8,128)(2,1)} %all-gather.3.cloned.1.call-done), kind=kOutput, calls=%fused_computation.7 | convolution fusion | flops 6443237376 | bytes 16252928 | tf_op jit(solution)/shard_map/dot_general | solution.py:108
  123.3 1.9 collective-permute-start
  125.1 3.7 %collective-permute-start.1 = (bf16[1,272,512]{2,1,0:T(8,128)(2,1)S(1)}, bf16[1,272,512]{2,1,0:T(8,128)(2,1)S(1)}, u32[]{:S(2)}, u32[]{:S(2)}) collective-permute-start(bf16[1,272,512]{2,1,0:T(8,128)(2,1)S(1)} %pad_maximum_fusion), channel_id=1, source_target_pairs={{0,16},{8,24},{16,32},{24,40},{32,48},{40,56},{48,64},{56,72},{64,... | collective-permute-start | bytes 835592 | tf_op jit(solution)/shard_map/ppermute | solution.py:27
  128.9 2.4 collective-permute-done
  133.1 4.3 %collective-permute-done.1 = bf16[1,272,512]{2,1,0:T(8,128)(2,1)S(1)} collective-permute-done((bf16[1,272,512]{2,1,0:T(8,128)(2,1)S(1)}, bf16[1,272,512]{2,1,0:T(8,128)(2,1)S(1)}, u32[]{:S(2)}, u32[]{:S(2)}) %collective-permute-start.1) | collective-permute-done | bytes 278560 | tf_op jit(solution)/shard_map/ppermute | solution.py:27
  140.7 5.6 %collective-permute-start.2 = (bf16[1,272,512]{2,1,0:T(8,128)(2,1)S(1)}, bf16[1,272,512]{2,1,0:T(8,128)(2,1)S(1)}, u32[]{:S(2)}, u32[]{:S(2)}) collective-permute-start(bf16[1,272,512]{2,1,0:T(8,128)(2,1)S(1)} %pad_maximum_fusion.1), channel_id=1, source_target_pairs={{0,16},{8,24},{16,32},{24,40},{32,48},{40,56},{48,64},{56,72},{64,... | collective-permute-start | bytes 835592 | tf_op jit(solution)/shard_map/ppermute | solution.py:27
  146.3 4.9 %collective-permute-done.2 = bf16[1,272,512]{2,1,0:T(8,128)(2,1)S(1)} collective-permute-done((bf16[1,272,512]{2,1,0:T(8,128)(2,1)S(1)}, bf16[1,272,512]{2,1,0:T(8,128)(2,1)S(1)}, u32[]{:S(2)}, u32[]{:S(2)}) %collective-permute-start.2) | collective-permute-done | bytes 278560 | tf_op jit(solution)/shard_map/ppermute | solution.py:27
  154.6 4.7 %collective-permute-start.3 = (bf16[1,272,512]{2,1,0:T(8,128)(2,1)S(1)}, bf16[1,272,512]{2,1,0:T(8,128)(2,1)S(1)}, u32[]{:S(2)}, u32[]{:S(2)}) collective-permute-start(bf16[1,272,512]{2,1,0:T(8,128)(2,1)S(1)} %pad_maximum_fusion.2), channel_id=1, source_target_pairs={{0,32},{8,40},{16,48},{24,56},{32,64},{40,72},{48,80},{56,88},{64,... | collective-permute-start | bytes 835592 | tf_op jit(solution)/shard_map/ppermute | solution.py:27
  159.3 3.5 %collective-permute-done.3 = bf16[1,272,512]{2,1,0:T(8,128)(2,1)S(1)} collective-permute-done((bf16[1,272,512]{2,1,0:T(8,128)(2,1)S(1)}, bf16[1,272,512]{2,1,0:T(8,128)(2,1)S(1)}, u32[]{:S(2)}, u32[]{:S(2)}) %collective-permute-start.3) | collective-permute-done | bytes 278560 | tf_op jit(solution)/shard_map/ppermute | solution.py:27
  166.2 5.7 %collective-permute-start.4 = (bf16[1,272,512]{2,1,0:T(8,128)(2,1)S(1)}, bf16[1,272,512]{2,1,0:T(8,128)(2,1)S(1)}, u32[]{:S(2)}, u32[]{:S(2)}) collective-permute-start(bf16[1,272,512]{2,1,0:T(8,128)(2,1)S(1)} %pad_maximum_fusion.3), channel_id=1, source_target_pairs={{0,64},{8,72},{16,80},{24,88},{32,96},{40,104},{48,112},{56,120},{... | collective-permute-start | bytes 835592 | tf_op jit(solution)/shard_map/ppermute | solution.py:27
  171.9 4.0 %collective-permute-done.4 = bf16[1,272,512]{2,1,0:T(8,128)(2,1)S(1)} collective-permute-done((bf16[1,272,512]{2,1,0:T(8,128)(2,1)S(1)}, bf16[1,272,512]{2,1,0:T(8,128)(2,1)S(1)}, u32[]{:S(2)}, u32[]{:S(2)}) %collective-permute-start.4) | collective-permute-done | bytes 278560 | tf_op jit(solution)/shard_map/ppermute | solution.py:27
  179.4 17.8 %collective-permute-start.5 = (bf16[1,272,512]{2,1,0:T(8,128)(2,1)S(1)}, bf16[1,272,512]{2,1,0:T(8,128)(2,1)S(1)}, u32[]{:S(2)}, u32[]{:S(2)}) collective-permute-start(bf16[1,272,512]{2,1,0:T(8,128)(2,1)S(1)} %pad_maximum_fusion.4), channel_id=1, source_target_pairs={{0,128},{8,136},{16,144},{24,152},{32,160},{40,168},{48,176},{56,1... | collective-permute-start | bytes 835592 | tf_op jit(solution)/shard_map/ppermute | solution.py:27
  197.2 4.0 %fusion.5 = f32[768,512]{0,1:T(8,128)} fusion(f32[768]{0:T(1024)S(1)} %multiply_reduce_fusion.1, f32[768]{0:T(1024)S(1)} %get-tuple-element.143, s32[768]{0:T(1024)S(1)} %get-tuple-element.142, bf16[768,1024]{1,0:T(8,128)(2,1)} %copy-done.3), kind=kOutput, calls=%fused_computation.15 | convolution fusion | flops 911867904 | bytes 3166208 | tf_op jit(solution)/shard_map/dot_general | solution.py:65
  201.2 1.8 collective-permute-done.5
  203.7 3.6 %fusion.52 = (f32[768]{0:T(1024)S(1)}, f32[768,512]{0,1:T(8,128)S(1)}) fusion(f32[768,512]{0,1:T(8,128)} %fusion.5, bf16[1,272,512]{2,1,0:T(8,128)(2,1)} %copy-done.2, f32[]{:T(128)} %bitcast.26, bf16[1,272,512]{2,1,0:T(8,128)(2,1)S(1)} %collective-permute-done.3, f32[]{:T(128)} %bitcast.22, bf16[1,272,512]{2,1,0:T(8,128)(2,1)} %copy-done.1, f32[]{:T(128)} %bitcast.27, ...), kind=kOutput, calls=%fused_computation.85 | convolution fusion | flops 1211235584 | bytes 5121536 | tf_op jit(solution)/shard_map/dot_general | solution.py:80
  207.6 10.5 %all-gather.5.cloned.1.call-done = bf16[512,4096]{1,0:T(8,128)(2,1)} async-done(((bf16[512,128]{1,0:T(8,128)(2,1)}), bf16[512,4096]{1,0:T(8,128)(2,1)}) %all-gather.5.cloned.1.call-update) | async-done | bytes 4194320 | tf_op jit(solution)/shard_map/all_gather | solution.py:141
  218.0 7.7 %convolution_convert_fusion = bf16[768,4096]{1,0:T(8,128)(2,1)} fusion(bf16[512,4096]{1,0:T(8,128)(2,1)} %all-gather.5.cloned.1.call-done, f32[768,512]{0,1:T(8,128)S(1)} %get-tuple-element.157, f32[512]{0:T(512)S(1)} %copy-done.7, f32[768]{0:T(1024)S(1)} %add_rsqrt_fusion, f32[768]{0:T(1024)S(1)} %broadcast_multiply_fusion), kind=kOutput, calls=%fused_computation | convolution fusion | flops 3225944064 | bytes 12066816 | tf_op jit(solution)/shard_map/dot_general | solution.py:143
  225.8 49.7 %reduce-scatter.2.cloned.1.call-done = bf16[96,4096]{1,0:T(8,128)(2,1)} async-done(((bf16[768,4096]{1,0:T(8,128)(2,1)}), bf16[96,4096]{1,0:T(8,128)(2,1)}) %reduce-scatter.2.cloned.1.call-update) | async-done | bytes 786448 | tf_op jit(solution)/shard_map/reduce_scatter | solution.py:142
  275.5 2.2 fusion.4
  (69 shorter events, 18.4 us)
Async XLA Ops:
  6.5 2.1 copy-start
  6.5 105.2 %all-gather.3.cloned.1.call-start = ((), (), s32[]{:S(2)}) async-start(), calls=%async_computation.2 | async-start | bytes 8650752 | tf_op jit(solution)/shard_map/all_gather | solution.py:107
  13.0 9.5 %copy-start.6 = (s32[1,768]{1,0:T(1,128)S(1)}, s32[1,768]{1,0:T(1,128)}, u32[]{:S(2)}) copy-start(s32[1,768]{1,0:T(1,128)} %param.39) | copy-start | bytes 9220
  13.0 9.9 %copy-start.4 = (s32[768]{0:T(1024)S(1)}, s32[768]{0:T(1024)}, u32[]{:S(2)}) copy-start(s32[768]{0:T(1024)} %param.41) | copy-start | bytes 9220
  13.0 15.1 %copy-start.5 = (s32[1,768]{1,0:T(1,128)S(1)}, s32[1,768]{1,0:T(1,128)}, u32[]{:S(2)}) copy-start(s32[1,768]{1,0:T(1,128)} %param.38) | copy-start | bytes 9220
  13.0 79.4 %all-to-all-start = ((bf16[8,96,4096]{2,1,0:T(8,128)(2,1)}), bf16[8,96,4096]{2,1,0:T(8,128)(2,1)}, u32[]{:S(2)}, u32[]{:S(2)}) async-start(bf16[8,96,4096]{2,1,0:T(8,128)(2,1)} %broadcast_in_dim.5), calls=%async_computation | async-start | bytes 12582912 | tf_op jit(solution)/shard_map/all_to_all | solution.py:106
  21.1 197.0 %all-gather.5.cloned.1.call-start = ((), (), s32[]{:S(2)}) async-start(), calls=%async_computation.3 | async-start | bytes 4325376 | tf_op jit(solution)/shard_map/all_gather | solution.py:141
  21.8 253.7 %reduce-scatter.2.cloned.1.call-start = ((), (), s32[]{:S(2)}) async-start(), calls=%async_computation.4 | async-start | bytes 7077888 | tf_op jit(solution)/shard_map/reduce_scatter | solution.py:142
  122.6 14.7 %copy-start.3 = (bf16[768,1024]{1,0:T(8,128)(2,1)}, bf16[768,1024]{1,0:T(8,128)(2,1)S(1)}, u32[]{:S(2)}) copy-start(bf16[768,1024]{1,0:T(8,128)(2,1)S(1)} %convolution_convert_fusion.1) | copy-start | bytes 4718596
  123.3 8.0 %collective-permute-start = (bf16[1,272,512]{2,1,0:T(8,128)(2,1)S(1)}, bf16[1,272,512]{2,1,0:T(8,128)(2,1)S(1)}, u32[]{:S(2)}, u32[]{:S(2)}) collective-permute-start(bf16[1,272,512]{2,1,0:T(8,128)(2,1)S(1)} %pad_maximum_fusion), channel_id=1, source_target_pairs={{0,8},{8,16},{16,24},{24,32},{32,40},{40,48},{48,56},{56,64},{64,7... | collective-permute-start | bytes 835592 | tf_op jit(solution)/shard_map/ppermute | solution.py:27
  125.1 12.3 %collective-permute-start.1 = (bf16[1,272,512]{2,1,0:T(8,128)(2,1)S(1)}, bf16[1,272,512]{2,1,0:T(8,128)(2,1)S(1)}, u32[]{:S(2)}, u32[]{:S(2)}) collective-permute-start(bf16[1,272,512]{2,1,0:T(8,128)(2,1)S(1)} %pad_maximum_fusion), channel_id=1, source_target_pairs={{0,16},{8,24},{16,32},{24,40},{32,48},{40,56},{48,64},{56,72},{64,... | collective-permute-start | bytes 835592 | tf_op jit(solution)/shard_map/ppermute | solution.py:27
  140.7 10.5 %collective-permute-start.2 = (bf16[1,272,512]{2,1,0:T(8,128)(2,1)S(1)}, bf16[1,272,512]{2,1,0:T(8,128)(2,1)S(1)}, u32[]{:S(2)}, u32[]{:S(2)}) collective-permute-start(bf16[1,272,512]{2,1,0:T(8,128)(2,1)S(1)} %pad_maximum_fusion.1), channel_id=1, source_target_pairs={{0,16},{8,24},{16,32},{24,40},{32,48},{40,56},{48,64},{56,72},{64,... | collective-permute-start | bytes 835592 | tf_op jit(solution)/shard_map/ppermute | solution.py:27
  154.6 8.2 %collective-permute-start.3 = (bf16[1,272,512]{2,1,0:T(8,128)(2,1)S(1)}, bf16[1,272,512]{2,1,0:T(8,128)(2,1)S(1)}, u32[]{:S(2)}, u32[]{:S(2)}) collective-permute-start(bf16[1,272,512]{2,1,0:T(8,128)(2,1)S(1)} %pad_maximum_fusion.2), channel_id=1, source_target_pairs={{0,32},{8,40},{16,48},{24,56},{32,64},{40,72},{48,80},{56,88},{64,... | collective-permute-start | bytes 835592 | tf_op jit(solution)/shard_map/ppermute | solution.py:27
  166.2 9.7 %collective-permute-start.4 = (bf16[1,272,512]{2,1,0:T(8,128)(2,1)S(1)}, bf16[1,272,512]{2,1,0:T(8,128)(2,1)S(1)}, u32[]{:S(2)}, u32[]{:S(2)}) collective-permute-start(bf16[1,272,512]{2,1,0:T(8,128)(2,1)S(1)} %pad_maximum_fusion.3), channel_id=1, source_target_pairs={{0,64},{8,72},{16,80},{24,88},{32,96},{40,104},{48,112},{56,120},{... | collective-permute-start | bytes 835592 | tf_op jit(solution)/shard_map/ppermute | solution.py:27
  175.9 25.3 %copy-start.1 = (bf16[1,272,512]{2,1,0:T(8,128)(2,1)}, bf16[1,272,512]{2,1,0:T(8,128)(2,1)S(1)}, u32[]{:S(2)}) copy-start(bf16[1,272,512]{2,1,0:T(8,128)(2,1)S(1)} %collective-permute-done.4) | copy-start | bytes 835588
  179.4 23.6 %collective-permute-start.5 = (bf16[1,272,512]{2,1,0:T(8,128)(2,1)S(1)}, bf16[1,272,512]{2,1,0:T(8,128)(2,1)S(1)}, u32[]{:S(2)}, u32[]{:S(2)}) collective-permute-start(bf16[1,272,512]{2,1,0:T(8,128)(2,1)S(1)} %pad_maximum_fusion.4), channel_id=1, source_target_pairs={{0,128},{8,136},{16,144},{24,152},{32,160},{40,168},{48,176},{56,1... | collective-permute-start | bytes 835592 | tf_op jit(solution)/shard_map/ppermute | solution.py:27
  203.0 0.7 copy-start.2
  207.3 10.7 %copy-start.7 = (f32[512]{0:T(512)S(1)}, f32[512]{0:T(512)}, u32[]{:S(2)}) copy-start(f32[512]{0:T(512)} %param.37) | copy-start | bytes 6148
Sparse Core Ops, SparseCore 0:
  9.9 101.7 all-gather.2
  114.2 103.7 all-gather.4
  225.9 49.5 reduce-scatter.1
where the time goes:
time: 285 us; the launch traced here: 284 us
  waiting for transfers between devices  165 us (58%)
  starting transfers between devices  47.5 us (17%)
  matrix products  26.8 us (9%)
  between operations  21.9 us (8%)
  local copies, waits for them, and re-layouts  15.7 us (6%)
  other arithmetic  7.54 us (3%)
    all_to_all x1, waiting for transfers between devices, local(): lax.all_to_all(copies, 'tp', 0, 0, tiled=True).reshape(-1, normed.shape[1])  63 us
    reduce_scatter x1, waiting for transfers between devices, local(): lax.psum_scatter(jnp.dot(normed_heads, out_columns, preferred_element_typ...  49.7 us
    ppermute x6, starting transfers between devices, shifted(): got = lax.ppermute(message, axis, pairs)  39.4 us
    ppermute x6, waiting for transfers between devices, shifted(): got = lax.ppermute(message, axis, pairs)  20.9 us
    all_gather x1, waiting for transfers between devices, local(): parameter_collection = lax.all_gather(w_qkv, 'ctx', axis=0, tiled=True)  19.3 us
    dot_general x1, matrix products, local(): jnp.dot(every_row_list, parameter_collection, preferred_element_type=jnp....  10.9 us
    all_gather x1, waiting for transfers between devices, local(): out_columns = lax.all_gather(w_out, 'ctx', axis=1, tiled=True)  10.5 us
    all_to_all x1, starting transfers between devices, local(): lax.all_to_all(copies, 'tp', 0, 0, tiled=True).reshape(-1, normed.shape[1])  8.05 us
  transfers between devices with their start and end apart: 10, of which 10 were waited for; matrix products, arithmetic and copies ran while one was open for 14% of the time, Pallas kernels for 0%

commit v1 on v0

--- a/solution.py
+++ b/solution.py
@@ -104,7 +104,9 @@
     group = lax.axis_size("tp")
     copies = jnp.broadcast_to(normed[None], (group,) + normed.shape)
     every_row_list = lax.all_to_all(copies, "tp", 0, 0, tiled=True).reshape(-1, normed.shape[1])
-    parameter_collection = lax.all_gather(w_qkv, "ctx", axis=0, tiled=True)
+    parameter_collection = jnp.concatenate(
+        lax.all_to_all(jnp.stack([w_qkv] * lax.axis_size("ctx")), "ctx", 0, 0), axis=0
+    )
     rows_combined = jnp.dot(
         every_row_list, parameter_collection, preferred_element_type=jnp.float32
     )

time: 285 us -> 480 us (1.68)
  waiting for transfers between devices: 165 us -> 280 us
  blocking collectives: 0 us -> 78.8 us
    all_to_all x1, waiting for transfers between devices: 63 us -> 197 us  [local(): lax.all_to_all(jnp.stack([w_qkv] * lax.axis_size('ctx')), 'ctx', 0, 0)]
    all_to_all x0 -> x1, blocking collectives: none -> 78.8 us  [local(): lax.all_to_all(copies, 'tp', 0, 0, tiled=True).reshape(-1, normed.shape[1])]
    all_gather x1 -> x0, waiting for transfers between devices: 19.3 us -> none  [local(): parameter_collection = lax.all_gather(w_qkv, 'ctx', axis=0, tiled=True)]
    reduce_scatter x1, waiting for transfers between devices: 49.7 us -> 64 us  [local(): lax.psum_scatter(jnp.dot(normed_heads, out_columns, preferred_element_typ...]
    all_gather x1, waiting for transfers between devices: 10.5 us -> 0.02 us  [local(): out_columns = lax.all_gather(w_out, 'ctx', axis=1, tiled=True)]
  transfers between devices with their start and end apart: 10 -> 9, of which waited for: 10 -> 7; matrix products, arithmetic and copies ran while one was open for 14% -> 7% of each run, Pallas kernels for 0% -> 0%
where the time goes in v1:
time: 480 us; the launch traced here: 479 us
  waiting for transfers between devices  280 us (58%)
  blocking collectives  78.8 us (16%)
  starting transfers between devices  46.6 us (10%)
  matrix products  26.6 us (6%)
  between operations  22.2 us (5%)
  local copies, waits for them, and re-layouts  17.5 us (4%)
  other arithmetic  7.94 us (2%)
    all_to_all x1, waiting for transfers between devices, local(): lax.all_to_all(jnp.stack([w_qkv] * lax.axis_size('ctx')), 'ctx', 0, 0)  197 us
    all_to_all x1, blocking collectives, local(): lax.all_to_all(copies, 'tp', 0, 0, tiled=True).reshape(-1, normed.shape[1])  78.8 us
    reduce_scatter x1, waiting for transfers between devices, local(): lax.psum_scatter(jnp.dot(normed_heads, out_columns, preferred_element_typ...  64 us
    ppermute x6, starting transfers between devices, shifted(): got = lax.ppermute(message, axis, pairs)  35.9 us
    ppermute x6, waiting for transfers between devices, shifted(): got = lax.ppermute(message, axis, pairs)  17.6 us
    dot_general x1, matrix products, local(): jnp.dot(every_row_list, parameter_collection, preferred_element_type=jnp....  10.9 us
    all_to_all x1, starting transfers between devices, local(): lax.all_to_all(jnp.stack([w_qkv] * lax.axis_size('ctx')), 'ctx', 0, 0)  10.6 us
  transfers between devices with their start and end apart: 9, of which 7 were waited for; matrix products, arithmetic and copies ran while one was open for 7% of the time, Pallas kernels for 0%

profile of v1, /device:TPU:1, one launch (start us, length us, event | category | flops | bytes accessed | tf_op | source)
XLA Modules:
  0.0 479.4 jit_solution(3667016658250359177)
XLA Ops:
  6.5 1.4 fusion.1
  7.9 1.4 fusion.3
  10.1 78.8 %all_to_all.10 = bf16[8,96,4096]{2,1,0:T(8,128)(2,1)} all-to-all(bf16[8,96,4096]{2,1,0:T(8,128)(2,1)S(1)} %broadcast_in_dim.5), channel_id=1, replica_groups=mesh['ctx'=32,'tp'=8] {'tp'}, dimensions={0} | all-to-all | bytes 12582912 | tf_op jit(solution)/shard_map/all_to_all | solution.py:106
  89.0 4.3 stack.4
  93.3 10.6 %all-to-all-start.1 = ((bf16[32,128,1024]{2,1,0:T(8,128)(2,1)}), bf16[32,128,1024]{2,1,0:T(8,128)(2,1)}, u32[]{:S(2)}, u32[]{:S(2)}) async-start(bf16[32,128,1024]{2,1,0:T(8,128)(2,1)} %stack.4), calls=%async_computation.1 | async-start | bytes 16777216 | tf_op jit(solution)/shard_map/all_to_all | solution.py:108
  112.2 197.5 %all-to-all-done.1 = bf16[32,128,1024]{2,1,0:T(8,128)(2,1)} async-done(((bf16[32,128,1024]{2,1,0:T(8,128)(2,1)}), bf16[32,128,1024]{2,1,0:T(8,128)(2,1)}, u32[]{:S(2)}, u32[]{:S(2)}) %all-to-all-start.1) | async-done | bytes 8388640 | tf_op jit(solution)/shard_map/all_to_all | solution.py:108
  309.7 10.9 %convolution_convert_fusion.1 = bf16[768,1024]{1,0:T(8,128)(2,1)S(1)} fusion(bf16[768,4096]{1,0:T(8,128)(2,1)} %bitcast.61, bf16[4096,1024]{1,0:T(8,128)(2,1)} %bitcast.1), kind=kOutput, calls=%fused_computation.7 | convolution fusion | flops 6443237376 | bytes 16252928 | tf_op jit(solution)/shard_map/dot_general | solution.py:110
  321.2 9.3 %collective-permute-start = (bf16[1,272,512]{2,1,0:T(8,128)(2,1)S(1)}, bf16[1,272,512]{2,1,0:T(8,128)(2,1)S(1)}, u32[]{:S(2)}, u32[]{:S(2)}) collective-permute-start(bf16[1,272,512]{2,1,0:T(8,128)(2,1)S(1)} %pad_maximum_fusion), channel_id=1, source_target_pairs={{0,8},{8,16},{16,24},{24,32},{32,40},{40,48},{48,56},{56,64},{64,7... | collective-permute-start | bytes 835592 | tf_op jit(solution)/shard_map/ppermute | solution.py:27
  330.5 3.6 collective-permute-start.1
  334.1 1.9 collective-permute-done
  337.9 4.1 collective-permute-done.1
  345.3 5.6 %collective-permute-start.2 = (bf16[1,272,512]{2,1,0:T(8,128)(2,1)S(1)}, bf16[1,272,512]{2,1,0:T(8,128)(2,1)S(1)}, u32[]{:S(2)}, u32[]{:S(2)}) collective-permute-start(bf16[1,272,512]{2,1,0:T(8,128)(2,1)S(1)} %pad_maximum_fusion.1), channel_id=1, source_target_pairs={{0,16},{8,24},{16,32},{24,40},{32,48},{40,56},{48,64},{56,72},{64,... | collective-permute-start | bytes 835592 | tf_op jit(solution)/shard_map/ppermute | solution.py:27
  351.0 4.6 collective-permute-done.2
  359.0 3.9 collective-permute-start.3
  362.9 3.5 collective-permute-done.3
  368.3 1.3 scatter.45
  369.8 3.6 collective-permute-start.4
  373.4 3.5 collective-permute-done.4
  380.5 10.0 %collective-permute-start.5 = (bf16[1,272,512]{2,1,0:T(8,128)(2,1)S(1)}, bf16[1,272,512]{2,1,0:T(8,128)(2,1)S(1)}, u32[]{:S(2)}, u32[]{:S(2)}) collective-permute-start(bf16[1,272,512]{2,1,0:T(8,128)(2,1)S(1)} %pad_maximum_fusion.4), channel_id=1, source_target_pairs={{0,128},{8,136},{16,144},{24,152},{32,160},{40,168},{48,176},{56,1... | collective-permute-start | bytes 835592 | tf_op jit(solution)/shard_map/ppermute | solution.py:27
  390.5 3.9 fusion.5
  394.4 3.4 fusion.52
  398.5 7.7 %convolution_convert_fusion = bf16[768,4096]{1,0:T(8,128)(2,1)} fusion(bf16[512,4096]{1,0:T(8,128)(2,1)} %all-gather.2.cloned.1.call-done, f32[768,512]{0,1:T(8,128)S(1)} %get-tuple-element.157, f32[512]{0:T(512)S(1)} %copy-done.6, f32[768]{0:T(1024)S(1)} %add_rsqrt_fusion, f32[768]{0:T(1024)S(1)} %broadcast_multiply_fusion), kind=kOutput, calls=%fused_computation | convolution fusion | flops 3225944064 | bytes 12066816 | tf_op jit(solution)/shard_map/dot_general | solution.py:145
  406.3 64.0 %reduce-scatter.2.cloned.1.call-done = bf16[96,4096]{1,0:T(8,128)(2,1)} async-done(((bf16[768,4096]{1,0:T(8,128)(2,1)}), bf16[96,4096]{1,0:T(8,128)(2,1)}) %reduce-scatter.2.cloned.1.call-update) | async-done | bytes 786448 | tf_op jit(solution)/shard_map/reduce_scatter | solution.py:144
  470.3 2.2 fusion.4
  (66 shorter events, 16.2 us)
Async XLA Ops:
  10.1 78.8 %copy-start.1 = (bf16[128,1024]{1,0:T(8,128)(2,1)S(1)}, bf16[128,1024]{1,0:T(8,128)(2,1)}, u32[]{:S(2)}) copy-start(bf16[128,1024]{1,0:T(8,128)(2,1)} %param.35) | copy-start | bytes 786436
  93.2 12.0 %copy-start.5 = (s32[1,768]{1,0:T(1,128)S(1)}, s32[1,768]{1,0:T(1,128)}, u32[]{:S(2)}) copy-start(s32[1,768]{1,0:T(1,128)} %param.39) | copy-start | bytes 9220
  93.3 12.5 %copy-start.3 = (s32[768]{0:T(1024)S(1)}, s32[768]{0:T(1024)}, u32[]{:S(2)}) copy-start(s32[768]{0:T(1024)} %param.41) | copy-start | bytes 9220
  93.3 17.6 %copy-start.4 = (s32[1,768]{1,0:T(1,128)S(1)}, s32[1,768]{1,0:T(1,128)}, u32[]{:S(2)}) copy-start(s32[1,768]{1,0:T(1,128)} %param.38) | copy-start | bytes 9220
  93.3 216.4 %all-to-all-start.1 = ((bf16[32,128,1024]{2,1,0:T(8,128)(2,1)}), bf16[32,128,1024]{2,1,0:T(8,128)(2,1)}, u32[]{:S(2)}, u32[]{:S(2)}) async-start(bf16[32,128,1024]{2,1,0:T(8,128)(2,1)} %stack.4), calls=%async_computation.1 | async-start | bytes 16777216 | tf_op jit(solution)/shard_map/all_to_all | solution.py:108
  103.9 294.2 %all-gather.2.cloned.1.call-start = ((), (), s32[]{:S(2)}) async-start(), calls=%async_computation.3 | async-start | bytes 4325376 | tf_op jit(solution)/shard_map/all_gather | solution.py:143
  104.6 365.7 %reduce-scatter.2.cloned.1.call-start = ((), (), s32[]{:S(2)}) async-start(), calls=%async_computation.4 | async-start | bytes 7077888 | tf_op jit(solution)/shard_map/reduce_scatter | solution.py:144
  320.6 21.4 %copy-start.2 = (bf16[768,1024]{1,0:T(8,128)(2,1)}, bf16[768,1024]{1,0:T(8,128)(2,1)S(1)}, u32[]{:S(2)}) copy-start(bf16[768,1024]{1,0:T(8,128)(2,1)S(1)} %convolution_convert_fusion.1) | copy-start | bytes 4718596
  321.2 14.8 %collective-permute-start = (bf16[1,272,512]{2,1,0:T(8,128)(2,1)S(1)}, bf16[1,272,512]{2,1,0:T(8,128)(2,1)S(1)}, u32[]{:S(2)}, u32[]{:S(2)}) collective-permute-start(bf16[1,272,512]{2,1,0:T(8,128)(2,1)S(1)} %pad_maximum_fusion), channel_id=1, source_target_pairs={{0,8},{8,16},{16,24},{24,32},{32,40},{40,48},{48,56},{56,64},{64,7... | collective-permute-start | bytes 835592 | tf_op jit(solution)/shard_map/ppermute | solution.py:27
  330.5 11.5 %collective-permute-start.1 = (bf16[1,272,512]{2,1,0:T(8,128)(2,1)S(1)}, bf16[1,272,512]{2,1,0:T(8,128)(2,1)S(1)}, u32[]{:S(2)}, u32[]{:S(2)}) collective-permute-start(bf16[1,272,512]{2,1,0:T(8,128)(2,1)S(1)} %pad_maximum_fusion), channel_id=1, source_target_pairs={{0,16},{8,24},{16,32},{24,40},{32,48},{40,56},{48,64},{56,72},{64,... | collective-permute-start | bytes 835592 | tf_op jit(solution)/shard_map/ppermute | solution.py:27
  345.3 10.2 %collective-permute-start.2 = (bf16[1,272,512]{2,1,0:T(8,128)(2,1)S(1)}, bf16[1,272,512]{2,1,0:T(8,128)(2,1)S(1)}, u32[]{:S(2)}, u32[]{:S(2)}) collective-permute-start(bf16[1,272,512]{2,1,0:T(8,128)(2,1)S(1)} %pad_maximum_fusion.1), channel_id=1, source_target_pairs={{0,16},{8,24},{16,32},{24,40},{32,48},{40,56},{48,64},{56,72},{64,... | collective-permute-start | bytes 835592 | tf_op jit(solution)/shard_map/ppermute | solution.py:27
  359.0 7.3 %collective-permute-start.3 = (bf16[1,272,512]{2,1,0:T(8,128)(2,1)S(1)}, bf16[1,272,512]{2,1,0:T(8,128)(2,1)S(1)}, u32[]{:S(2)}, u32[]{:S(2)}) collective-permute-start(bf16[1,272,512]{2,1,0:T(8,128)(2,1)S(1)} %pad_maximum_fusion.2), channel_id=1, source_target_pairs={{0,32},{8,40},{16,48},{24,56},{32,64},{40,72},{48,80},{56,88},{64,... | collective-permute-start | bytes 835592 | tf_op jit(solution)/shard_map/ppermute | solution.py:27
  369.8 7.1 %collective-permute-start.4 = (bf16[1,272,512]{2,1,0:T(8,128)(2,1)S(1)}, bf16[1,272,512]{2,1,0:T(8,128)(2,1)S(1)}, u32[]{:S(2)}, u32[]{:S(2)}) collective-permute-start(bf16[1,272,512]{2,1,0:T(8,128)(2,1)S(1)} %pad_maximum_fusion.3), channel_id=1, source_target_pairs={{0,64},{8,72},{16,80},{24,88},{32,96},{40,104},{48,112},{56,120},{... | collective-permute-start | bytes 835592 | tf_op jit(solution)/shard_map/ppermute | solution.py:27
  380.5 13.9 %collective-permute-start.5 = (bf16[1,272,512]{2,1,0:T(8,128)(2,1)S(1)}, bf16[1,272,512]{2,1,0:T(8,128)(2,1)S(1)}, u32[]{:S(2)}, u32[]{:S(2)}) collective-permute-start(bf16[1,272,512]{2,1,0:T(8,128)(2,1)S(1)} %pad_maximum_fusion.4), channel_id=1, source_target_pairs={{0,128},{8,136},{16,144},{24,152},{32,160},{40,168},{48,176},{56,1... | collective-permute-start | bytes 835592 | tf_op jit(solution)/shard_map/ppermute | solution.py:27
  397.8 0.7 copy-start.6
  406.3 64.1 %copy-start = (bf16[96,4096]{1,0:T(8,128)(2,1)S(1)}, bf16[96,4096]{1,0:T(8,128)(2,1)}, u32[]{:S(2)}) copy-start(bf16[96,4096]{1,0:T(8,128)(2,1)} %param.33) | copy-start | bytes 2359300
Sparse Core Ops, SparseCore 0:
  107.2 193.1 all-gather.1
  406.4 63.8 reduce-scatter.1
